TPU v7x, 32 devices: a whole 2x2x4 slice. The times are simulated.
32 devices in a mesh: tile: 8 (over z, y), date: 4 (over x, core).
Axes of the slice: x: 2, y: 2, z: 4, core: 2. Of those that a mesh axis runs over, the one named last changes fastest.
Arguments:
- complex_images: bfloat16 [8, 8, 8, 2, 10, 1920], P('date', 'tile')
- segment_position_map: int32 [8, 8], P('tile'), may hold values from 0 to 7, each once within a row
- usable_position_total: int32 [8], P('tile'), may hold values from 4 to 8
- interferogram_epochs: int32 [16, 2], replicated, may hold values from 0 to 7, as said below
Outputs:
- coherence: float32 [16, 2, 16, 1024], P('date', None, None, 'tile')
Inputs may be any that keep to these rules, and one draw needn't show every extreme that they name: Each row of segment_position_map names every block position once. `interferogram_epochs`: the two dates of a pair differ.
All inputs are finite; a program needn't handle non-finite values.
Results may differ from a plain program's by a relative error of at most 0.0003.
Values may be sent and summed in bfloat16 or wider, within the bound.
A program may use at most 128 MiB of HBM per device.

v0:
```python
import jax
import jax.numpy as jnp
from jax import lax
from jax.sharding import PartitionSpec as P

LOOK_RG = 15
LOOK_AZ = 5
EPS = 1e-05


def tile_looks(stack, first_idx, second_idx, valid, box):
    scale = 1.0 / (LOOK_AZ * LOOK_RG)

    def looks(values):
        ranged = jnp.dot(
            values, box, precision=lax.Precision.HIGHEST, preferred_element_type=jnp.float32
        )
        extent = ranged.shape
        return (
            ranged.reshape(extent[:-2] + (extent[-2] // LOOK_AZ, LOOK_AZ, extent[-1])).sum(axis=-2)
            * scale
        )

    def date_power(image):
        image = image.astype(jnp.float32)
        return looks(image[:, 0] * image[:, 0] + image[:, 1] * image[:, 1])

    power = lax.map(date_power, stack)

    def one_pair(indices):
        first = lax.dynamic_index_in_dim(stack, indices[0], 0, keepdims=False).astype(jnp.float32)
        second = lax.dynamic_index_in_dim(stack, indices[1], 0, keepdims=False).astype(jnp.float32)
        cross_re = looks(first[:, 0] * second[:, 0] + first[:, 1] * second[:, 1])
        cross_im = looks(first[:, 1] * second[:, 0] - first[:, 0] * second[:, 1])
        power_first = lax.dynamic_index_in_dim(power, indices[0], 0, keepdims=False)
        power_second = lax.dynamic_index_in_dim(power, indices[1], 0, keepdims=False)
        weight = valid[:, None, None] / jnp.sqrt((power_first + EPS) * (power_second + EPS))
        return jnp.stack([cross_re * weight, cross_im * weight], axis=0)

    return lax.map(one_pair, jnp.stack([first_idx, second_idx], axis=1))


def place_rows(gamma, positions):
    ranking = jnp.argsort(positions)
    placed = jnp.take(gamma, ranking, axis=2)
    extent = placed.shape
    return placed.reshape(extent[0], extent[1], extent[2] * extent[3], extent[4])


def on_device(complex_images, segment_position_map, usable_position_total, interferogram_epochs):
    groups = lax.axis_size("date")
    tile_cols = complex_images.shape[-1]
    box = (
        jnp.arange(tile_cols)[:, None] // LOOK_RG == jnp.arange(tile_cols // LOOK_RG)[None, :]
    ).astype(jnp.float32)
    positions = segment_position_map[0]
    moved = lax.all_to_all(complex_images, "tile", split_axis=2, concat_axis=1, tiled=True)
    stack = moved[:, :, 0]
    valid = (positions < usable_position_total[0]).astype(jnp.float32)
    gathered = lax.all_gather(stack, "date", axis=0, tiled=True)
    mine = interferogram_epochs.shape[0] // groups
    local_pairs = lax.dynamic_slice_in_dim(
        interferogram_epochs, lax.axis_index("date") * mine, mine, 0
    )
    gamma = tile_looks(gathered, local_pairs[:, 0], local_pairs[:, 1], valid, box)
    return place_rows(gamma, positions)


def solution(mesh):
    in_specs = (P("date", "tile", None, None, None, None), P("tile", None), P("tile"), P())
    out_specs = P("date", None, None, "tile")
    return jax.shard_map(
        on_device, mesh=mesh, in_specs=in_specs, out_specs=out_specs, check_vma=False
    )
```

profile of v0, /device:TPU:0, one launch (start us, length us, event | category | flops | bytes accessed | tf_op | source)
XLA Modules:
  0.0 142.8 jit_solution(7151218420765707386)
XLA Ops:
  6.5 2.1 %copy.19 = bf16[2,1,8,2,10,1920]{5,3,4,1,0,2:T(2,128)(2,1)S(1)} copy(bf16[2,1,8,2,10,1920]{5,3,4,2,1,0:T(2,128)(2,1)} %param.8) | data formatting | bytes 2457600 | tf_op args[0]
  8.7 36.9 %all_to_all.4 = bf16[2,1,8,2,10,1920]{5,3,4,1,0,2:T(2,128)(2,1)S(1)} all-to-all(bf16[2,1,8,2,10,1920]{5,3,4,1,0,2:T(2,128)(2,1)S(1)} %copy.19), channel_id=1, replica_groups=mesh['tile'=8,'date'=4] {'tile'}, dimensions={2} | all-to-all | bytes 2457600 | tf_op jit(solution)/shard_map/all_to_all | solution.py:57
  45.6 1.2 copy.20
  47.5 1.0 sort.17
  48.4 0.1 broadcast_in_dim.31
  48.5 0.1 broadcast_in_dim.32
  48.6 0.1 constant_dynamic-slice_fusion.1
  48.7 35.6 %all-gather.3.cloned.1.call-done = bf16[8,1,8,2,10,1920]{5,2,4,3,1,0:T(8,128)(2,1)} async-done(((bf16[2,1,8,2,10,1920]{5,2,4,3,1,0:T(8,128)(2,1)}), bf16[8,1,8,2,10,1920]{5,2,4,3,1,0:T(8,128)(2,1)}) %all-gather.3.cloned.1.call-update) | async-done | bytes 4915216 | tf_op jit(solution)/shard_map/all_gather | solution.py:60
  84.4 17.9 %while.23 = (s32[]{:T(128)}, f32[8,8,2,128]{3,1,2,0:T(8,128)S(1)}, bf16[8,8,2,10,1920]{4,1,3,2,0:T(8,128)(2,1)}, s32[1920]{0:T(1024)S(1)}, s32[]{:T(128)}) while((s32[]{:T(128)}, f32[8,8,2,128]{3,1,2,0:T(8,128)S(1)}, bf16[8,8,2,10,1920]{4,1,3,2,0:T(8,128)(2,1)}, s32[1920]{0:T(1024)S(1)}, s32[]{:T(128)}) %tuple.60), condition=%wide.region_3.4_spmd.clone, body=%wide.region_1.3_spmd.clone.sunk | while | flops 237199360 | bytes 4333125 | solution.py:28
  84.4 1.2 bitcast_convert_fusion.5
  85.5 0.1 fusion.31
  85.6 1.0 convolution_reduce_fusion.6
  86.6 1.2 bitcast_convert_fusion.5
  87.7 0.1 fusion.31
  87.8 1.0 convolution_reduce_fusion.6
  88.8 1.2 bitcast_convert_fusion.5
  90.1 1.0 convolution_reduce_fusion.6
  91.1 1.2 bitcast_convert_fusion.5
  92.2 0.1 fusion.31
  92.3 1.0 convolution_reduce_fusion.6
  93.3 1.2 bitcast_convert_fusion.5
  94.4 0.1 fusion.31
  94.5 1.0 convolution_reduce_fusion.6
  95.5 1.2 bitcast_convert_fusion.5
  96.8 1.0 convolution_reduce_fusion.6
  97.8 1.2 bitcast_convert_fusion.5
  99.0 1.0 convolution_reduce_fusion.6
  100.0 1.2 bitcast_convert_fusion.5
  101.2 1.0 convolution_reduce_fusion.6
  102.2 32.4 %while.24 = (s32[]{:T(128)}, f32[4,2,8,2,128]{4,0,3,2,1:T(4,128)S(1)}, s32[4,2]{0,1:T(2,128)S(1)}, bf16[8,8,2,10,1920]{4,1,3,2,0:T(8,128)(2,1)}, f32[8]{0:T(128)...) while((s32[]{:T(128)}, ...), condition=%wide.region_7.8_spmd.clone.clone, body=%wide.region_4.7_spmd.clone.clone.sunk | while | flops 474415104 | bytes 8781057 | solution.py:40
  102.2 0.1 constant_dynamic-slice_fusion.3
  102.3 0.6 fusion.36
  106.6 1.4 bitcast_convert_fusion.6
  108.0 0.1 multiply_add_fusion.2
  108.2 1.0 convolution_reduce_fusion.7
  109.1 1.0 convolution_reduce_fusion.8
  110.1 0.1 bitcast_multiply_fusion.3
  110.2 0.1 dynamic_update_slice.15
  110.3 0.1 constant_dynamic-slice_fusion.3
  110.4 0.6 fusion.36
  114.7 1.4 bitcast_convert_fusion.6
  116.1 0.1 multiply_add_fusion.2
  116.3 1.0 convolution_reduce_fusion.7
  117.2 1.0 convolution_reduce_fusion.8
  118.2 0.1 bitcast_multiply_fusion.3
  118.3 0.1 dynamic_update_slice.15
  118.4 0.1 constant_dynamic-slice_fusion.3
  118.5 0.6 fusion.36
  122.8 1.4 bitcast_convert_fusion.6
  124.2 0.1 multiply_add_fusion.2
  124.4 1.0 convolution_reduce_fusion.7
  125.3 1.0 convolution_reduce_fusion.8
  126.3 0.1 bitcast_multiply_fusion.3
  126.4 0.1 dynamic_update_slice.15
  126.5 0.1 constant_dynamic-slice_fusion.3
  126.6 0.6 fusion.36
  130.9 1.4 bitcast_convert_fusion.6
  132.3 0.1 multiply_add_fusion.2
  132.5 1.0 convolution_reduce_fusion.7
  133.4 1.0 convolution_reduce_fusion.8
  134.4 0.1 bitcast_multiply_fusion.3
  134.5 0.1 dynamic_update_slice.15
  134.6 0.6 gather_fusion
  135.2 0.7 broadcast_select_fusion
  (35 shorter events, 0.5 us)
Async XLA Ops:
  6.5 42.1 %copy-start = (s32[16,2]{0,1:T(2,128)S(1)}, s32[16,2]{0,1:T(2,128)}, u32[]{:S(2)}) copy-start(s32[16,2]{0,1:T(2,128)} %param.11) | copy-start | bytes 388
  6.5 77.8 %all-gather.3.cloned.1.call-start = ((), (), s32[]{:S(2)}) async-start(), calls=%async_computation.1 | async-start | bytes 6144000 | tf_op jit(solution)/shard_map/all_gather | solution.py:60
  46.7 0.7 copy-start.1
Sparse Core Ops, SparseCore 0:
  46.9 37.4 all-gather.2
where the time goes:
time: 144 us; the launch traced here: 143 us
  blocking collectives  36.9 us (26%)
  waiting for transfers between devices  35.6 us (25%)
  other arithmetic  18.1 us (13%)
  matrix products  15.4 us (11%)
  loops' own time  15.3 us (11%)
  between operations  14.1 us (10%)
  local copies, waits for them, and re-layouts  7.39 us (5%)
    all_to_all x1, blocking collectives, on_device(): lax.all_to_all(complex_images, 'tile', split_axis=2, concat_axis=1, tiled...  36.9 us
    all_gather x1, waiting for transfers between devices, on_device(): gathered = lax.all_gather(stack, 'date', axis=0, tiled=True)  35.6 us
    dot_general x16, matrix products, looks(): jnp.dot(values, box, precision=lax.Precision.HIGHEST, preferred_element_t...  15.4 us
    another operation x1, loops' own time, tile_looks(): return lax.map(one_pair, jnp.stack([first_idx, second_idx], axis=1))  15 us
    convert_element_type x8, other arithmetic, date_power(): image = image.astype(jnp.float32)  9.26 us
    convert_element_type x4, other arithmetic, one_pair(): lax.dynamic_index_in_dim(stack, indices[0], 0, keepdims=False)  5.7 us
  transfers between devices with their start and end apart: 1, of which 1 were waited for; matrix products, arithmetic and copies ran while one was open for 1% of the time, Pallas kernels for 0%

commit v1 on v0

--- a/solution.py
+++ b/solution.py
@@ -6,6 +6,22 @@
 LOOK_RG = 15
 LOOK_AZ = 5
 EPS = 1e-05
+
+
+def pairwise_exchange(x, axis, split, join):
+    ways, here = (lax.axis_size(axis), lax.axis_index(axis))
+    width = x.shape[split] // ways
+    shape = list(x.shape)
+    shape[split] = width
+    height = shape[join]
+    shape[join] = height * ways
+    full = jnp.zeros(shape, x.dtype)
+    for mask in range(ways):
+        part = lax.dynamic_slice_in_dim(x, (here ^ mask) * width, width, axis=split)
+        if mask:
+            part = lax.ppermute(part, axis, [(d, d ^ mask) for d in range(ways)])
+        full = lax.dynamic_update_slice_in_dim(full, part, (here ^ mask) * height, axis=join)
+    return full
 
 
 def tile_looks(stack, first_idx, second_idx, valid, box):
@@ -54,7 +70,7 @@
         jnp.arange(tile_cols)[:, None] // LOOK_RG == jnp.arange(tile_cols // LOOK_RG)[None, :]
     ).astype(jnp.float32)
     positions = segment_position_map[0]
-    moved = lax.all_to_all(complex_images, "tile", split_axis=2, concat_axis=1, tiled=True)
+    moved = pairwise_exchange(complex_images, "tile", 2, 1)
     stack = moved[:, :, 0]
     valid = (positions < usable_position_total[0]).astype(jnp.float32)
     gathered = lax.all_gather(stack, "date", axis=0, tiled=True)

time: 144 us -> 159 us (1.10)
  blocking collectives: 36.9 us -> 0 us
  local copies, waits for them, and re-layouts: 7.39 us -> 28.4 us
  waiting for transfers between devices: 35.6 us -> 52.7 us
  starting transfers between devices: 0.01 us -> 13.4 us
    all_to_all x1 -> x0, blocking collectives: 36.9 us -> none  [on_device(): lax.all_to_all(complex_images, 'tile', split_axis=2, concat_axis=1, tiled...]
    dynamic_update_slice x0 -> x8, local copies, waits for them, and re-layouts: none -> 17.4 us  [pairwise_exchange(): lax.dynamic_update_slice_in_dim(full, part, (here ^ mask) * height, axis=...]
    ppermute x0 -> x7, starting transfers between devices: none -> 13.4 us  [pairwise_exchange(): part = lax.ppermute(part, axis, [(d, d ^ mask) for d in range(ways)])]
    ppermute x0 -> x7, waiting for transfers between devices: none -> 13 us  [pairwise_exchange(): part = lax.ppermute(part, axis, [(d, d ^ mask) for d in range(ways)])]
    all_gather x1, waiting for transfers between devices: 35.6 us -> 39.7 us  [on_device(): gathered = lax.all_gather(stack, 'date', axis=0, tiled=True)]
    squeeze x0 -> x9, local copies, waits for them, and re-layouts: none -> 3.82 us  [on_device(): stack = moved[:, :, 0]]
    dynamic_slice x0 -> x1, local copies, waits for them, and re-layouts: none -> 2.21 us  [pairwise_exchange(): part = lax.dynamic_slice_in_dim(x, (here ^ mask) * width, width, axis=split)]
  transfers between devices with their start and end apart: 1 -> 8, of which waited for: 1 -> 3; matrix products, arithmetic and copies ran while one was open for 1% -> 4% of each run, Pallas kernels for 0% -> 0%
where the time goes in v1:
time: 159 us; the launch traced here: 158 us
  waiting for transfers between devices  52.7 us (33%)
  local copies, waits for them, and re-layouts  28.4 us (18%)
  other arithmetic  18.2 us (11%)
  loops' own time  15.4 us (10%)
  matrix products  15.4 us (10%)
  between operations  14.3 us (9%)
  starting transfers between devices  13.4 us (8%)
    all_gather x1, waiting for transfers between devices, on_device(): gathered = lax.all_gather(stack, 'date', axis=0, tiled=True)  39.7 us
    dynamic_update_slice x8, local copies, waits for them, and re-layouts, pairwise_exchange(): lax.dynamic_update_slice_in_dim(full, part, (here ^ mask) * height, axis=...  17.4 us
    dot_general x16, matrix products, looks(): jnp.dot(values, box, precision=lax.Precision.HIGHEST, preferred_element_t...  15.4 us
    another operation x1, loops' own time, tile_looks(): return lax.map(one_pair, jnp.stack([first_idx, second_idx], axis=1))  15.1 us
    ppermute x7, starting transfers between devices, pairwise_exchange(): part = lax.ppermute(part, axis, [(d, d ^ mask) for d in range(ways)])  13.4 us
    ppermute x7, waiting for transfers between devices, pairwise_exchange(): part = lax.ppermute(part, axis, [(d, d ^ mask) for d in range(ways)])  13 us
    convert_element_type x8, other arithmetic, date_power(): image = image.astype(jnp.float32)  9.26 us
    convert_element_type x4, other arithmetic, one_pair(): lax.dynamic_index_in_dim(stack, indices[0], 0, keepdims=False)  5.7 us
  transfers between devices with their start and end apart: 8, of which 3 were waited for; matrix products, arithmetic and copies ran while one was open for 4% of the time, Pallas kernels for 0%

profile of v1, /device:TPU:0, one launch (start us, length us, event | category | flops | bytes accessed | tf_op | source)
XLA Modules:
  0.0 157.7 jit_solution(13649408793435155503)
XLA Ops:
  6.5 2.2 %constant_dynamic-slice_fusion.1 = (bf16[2,1,1,2,10,1920]{5,3,4,2,1,0:T(2,128)(2,1)S(1)}, bf16[2,1,1,2,10,1920]{5,3,4,2,1,0:T(2,128)(2,1)S(1)}, bf16[2,1,1,2,10,...) fusion(bf16[2,1,8,2,10,1920]{5,3,4,2,1,0:T(2,128)(2,1)} %param., ...), kind=kLoop, calls=%fused_computation.42 | loop fusion | bytes 2457632 | tf_op jit(solution)/shard_map/dynamic_slice | solution.py:20
  8.8 3.1 %collective-permute-start = (bf16[2,1,1,2,10,1920]{5,3,4,2,1,0:T(2,128)(2,1)S(1)}, bf16[2,1,1,2,10,1920]{5,3,4,2,1,0:T(2,128)(2,1)S(1)}, u32[]{:S(2)}, u32[]{:S(2)}) collective-permute-start(bf16[2,1,1,2,10,1920]{5,3,4,2,1,0:T(2,128)(2,1)S(1)} %get-tuple-element.152), channel_id=1, source_target_pairs={{0,4},{4,0},{8,12},{12,8},{16,20},{20,16},{24,28},{28,24},{1,5},{5... | collective-permute-start | bytes 460808 | tf_op jit(solution)/shard_map/ppermute | solution.py:22
  11.8 1.6 collective-permute-start.1
  13.4 3.0 %collective-permute-start.3 = (bf16[2,1,1,2,10,1920]{5,3,4,2,1,0:T(2,128)(2,1)S(1)}, bf16[2,1,1,2,10,1920]{5,3,4,2,1,0:T(2,128)(2,1)S(1)}, u32[]{:S(2)}, u32[]{:S(2)}) collective-permute-start(bf16[2,1,1,2,10,1920]{5,3,4,2,1,0:T(2,128)(2,1)S(1)} %get-tuple-element.149), channel_id=1, source_target_pairs={{0,16},{4,20},{8,24},{12,28},{16,0},{20,4},{24,8},{28,12},{1,17},{... | collective-permute-start | bytes 460808 | tf_op jit(solution)/shard_map/ppermute | solution.py:22
  16.4 1.3 collective-permute-start.4
  17.7 3.6 %collective-permute-start.5 = (bf16[2,1,1,2,10,1920]{5,3,4,2,1,0:T(2,128)(2,1)S(1)}, bf16[2,1,1,2,10,1920]{5,3,4,2,1,0:T(2,128)(2,1)}, u32[]{:S(2)}, u32[]{:S(2)}) collective-permute-start(bf16[2,1,1,2,10,1920]{5,3,4,2,1,0:T(2,128)(2,1)S(1)} %get-tuple-element.154), channel_id=1, source_target_pairs={{0,24},{4,28},{8,16},{12,20},{16,8},{20,12},{24,0},{28,4},{1,25},{... | collective-permute-start | bytes 460808 | tf_op jit(solution)/shard_map/ppermute | solution.py:22
  21.3 2.9 %collective-permute-done.1 = bf16[2,1,1,2,10,1920]{5,3,4,2,1,0:T(2,128)(2,1)S(1)} collective-permute-done((bf16[2,1,1,2,10,1920]{5,3,4,2,1,0:T(2,128)(2,1)S(1)}, bf16[2,1,1,2,10,1920]{5,3,4,2,1,0:T(2,128)(2,1)S(1)}, u32[]{:S(2)}, u32[]{:S(2)}) %collective-permute-start.1) | collective-permute-done | bytes 153632 | tf_op jit(solution)/shard_map/ppermute | solution.py:22
  24.2 0.9 collective-permute-start.6
  25.1 0.2 copy.41
  25.5 2.2 %dynamic_update_slice.40 = bf16[2,8,2,10,1920]{4,1,3,2,0:T(8,128)(2,1)S(1)} dynamic-update-slice(bf16[2,8,2,10,1920]{4,1,3,2,0:T(8,128)(2,1)S(1)} %squeeze.56, bf16[2,1,2,10,1920]{4,1,3,2,0:T(2,128)(2,1)S(1)} %copy.41, s32[]{:T(128)} %constant.87.clone.1, s32[]{:T(128)S(6)} %select_n.71, s32[]{:T(128)} %constant.87.clone.1, s32[]{:T(128)} %constant.87.clone.1, s32[]{:T(128)} %constant.87.clone.1) | dynamic-update-slice | bytes 307204 | tf_op jit(solution)/shard_map/dynamic_update_slice | solution.py:23
  27.6 0.2 copy.42
  27.9 0.2 copy.43
  28.1 0.2 copy.44
  28.4 0.2 copy.45
  28.6 10.0 %collective-permute-done.4 = bf16[2,1,1,2,10,1920]{5,3,4,2,1,0:T(2,128)(2,1)S(1)} collective-permute-done((bf16[2,1,1,2,10,1920]{5,3,4,2,1,0:T(2,128)(2,1)S(1)}, bf16[2,1,1,2,10,1920]{5,3,4,2,1,0:T(2,128)(2,1)S(1)}, u32[]{:S(2)}, u32[]{:S(2)}) %collective-permute-start.4) | collective-permute-done | bytes 153632 | tf_op jit(solution)/shard_map/ppermute | solution.py:22
  38.7 0.2 copy.46
  38.9 1.2 copy.47
  40.1 1.2 copy.48
  41.2 2.2 %dynamic_update_slice.41 = bf16[2,8,2,10,1920]{4,1,3,2,0:T(8,128)(2,1)S(1)} dynamic-update-slice(bf16[2,8,2,10,1920]{4,1,3,2,0:T(8,128)(2,1)S(1)} %dynamic_update_slice.40, bf16[2,1,2,10,1920]{4,1,3,2,0:T(2,128)(2,1)S(1)} %copy.42, s32[]{:T(128)} %constant.87.clone.1, s32[]{:T(128)S(6)} %select_n.72, s32[]{:T(128)} %constant.87.clone.1, s32[]{:T(128)} %constant.87.clone.1, s32[]{:T(128)} %constant.87.clone.1) | dynamic-update-slice | bytes 307204 | tf_op jit(solution)/shard_map/dynamic_update_slice | solution.py:23
  43.4 2.2 %dynamic_update_slice.42 = bf16[2,8,2,10,1920]{4,1,3,2,0:T(8,128)(2,1)S(1)} dynamic-update-slice(bf16[2,8,2,10,1920]{4,1,3,2,0:T(8,128)(2,1)S(1)} %dynamic_update_slice.41, bf16[2,1,2,10,1920]{4,1,3,2,0:T(2,128)(2,1)S(1)} %copy.43, s32[]{:T(128)} %constant.87.clone.1, s32[]{:T(128)S(6)} %select_n.73, s32[]{:T(128)} %constant.87.clone.1, s32[]{:T(128)} %constant.87.clone.1, s32[]{:T(128)} %constant.87.clone.1) | dynamic-update-slice | bytes 307204 | tf_op jit(solution)/shard_map/dynamic_update_slice | solution.py:23
  45.6 2.2 %dynamic_update_slice.43 = bf16[2,8,2,10,1920]{4,1,3,2,0:T(8,128)(2,1)S(1)} dynamic-update-slice(bf16[2,8,2,10,1920]{4,1,3,2,0:T(8,128)(2,1)S(1)} %dynamic_update_slice.42, bf16[2,1,2,10,1920]{4,1,3,2,0:T(2,128)(2,1)S(1)} %copy.44, s32[]{:T(128)} %constant.87.clone.1, s32[]{:T(128)S(6)} %select_n.74, s32[]{:T(128)} %constant.87.clone.1, s32[]{:T(128)} %constant.87.clone.1, s32[]{:T(128)} %constant.87.clone.1) | dynamic-update-slice | bytes 307204 | tf_op jit(solution)/shard_map/dynamic_update_slice | solution.py:23
  47.8 2.2 %dynamic_update_slice.44 = bf16[2,8,2,10,1920]{4,1,3,2,0:T(8,128)(2,1)S(1)} dynamic-update-slice(bf16[2,8,2,10,1920]{4,1,3,2,0:T(8,128)(2,1)S(1)} %dynamic_update_slice.43, bf16[2,1,2,10,1920]{4,1,3,2,0:T(2,128)(2,1)S(1)} %copy.45, s32[]{:T(128)} %constant.87.clone.1, s32[]{:T(128)S(6)} %select_n.75, s32[]{:T(128)} %constant.87.clone.1, s32[]{:T(128)} %constant.87.clone.1, s32[]{:T(128)} %constant.87.clone.1) | dynamic-update-slice | bytes 307204 | tf_op jit(solution)/shard_map/dynamic_update_slice | solution.py:23
  50.0 2.2 %dynamic_update_slice.45 = bf16[2,8,2,10,1920]{4,1,3,2,0:T(8,128)(2,1)S(1)} dynamic-update-slice(bf16[2,8,2,10,1920]{4,1,3,2,0:T(8,128)(2,1)S(1)} %dynamic_update_slice.44, bf16[2,1,2,10,1920]{4,1,3,2,0:T(2,128)(2,1)S(1)} %copy.46, s32[]{:T(128)} %constant.87.clone.1, s32[]{:T(128)S(6)} %select_n.76, s32[]{:T(128)} %constant.87.clone.1, s32[]{:T(128)} %constant.87.clone.1, s32[]{:T(128)} %constant.87.clone.1) | dynamic-update-slice | bytes 307204 | tf_op jit(solution)/shard_map/dynamic_update_slice | solution.py:23
  52.2 2.2 %dynamic_update_slice.46 = bf16[2,8,2,10,1920]{4,1,3,2,0:T(8,128)(2,1)S(1)} dynamic-update-slice(bf16[2,8,2,10,1920]{4,1,3,2,0:T(8,128)(2,1)S(1)} %dynamic_update_slice.45, bf16[2,1,2,10,1920]{4,1,3,2,0:T(2,128)(2,1)S(1)} %copy.47, s32[]{:T(128)} %constant.87.clone.1, s32[]{:T(128)S(6)} %select_n.77, s32[]{:T(128)} %constant.87.clone.1, s32[]{:T(128)} %constant.87.clone.1, s32[]{:T(128)} %constant.87.clone.1) | dynamic-update-slice | bytes 307204 | tf_op jit(solution)/shard_map/dynamic_update_slice | solution.py:23
  54.4 2.2 %dynamic_update_slice.47 = bf16[2,8,2,10,1920]{4,1,3,2,0:T(8,128)(2,1)S(1)} dynamic-update-slice(bf16[2,8,2,10,1920]{4,1,3,2,0:T(8,128)(2,1)S(1)} %dynamic_update_slice.46, bf16[2,1,2,10,1920]{4,1,3,2,0:T(2,128)(2,1)S(1)} %copy.48, s32[]{:T(128)} %constant.87.clone.1, s32[]{:T(128)S(6)} %select_n.78, s32[]{:T(128)} %constant.87.clone.1, s32[]{:T(128)} %constant.87.clone.1, s32[]{:T(128)} %constant.87.clone.1) | dynamic-update-slice | bytes 307204 | tf_op jit(solution)/shard_map/dynamic_update_slice | solution.py:23
  56.5 1.0 copy-done.1
  58.3 1.0 sort.17
  59.6 39.7 %all-gather.2.cloned.1.call-done = bf16[8,8,2,10,1920]{4,1,3,2,0:T(8,128)(2,1)} async-done(((bf16[2,8,2,10,1920]{4,1,3,2,0:T(8,128)(2,1)}), bf16[8,8,2,10,1920]{4,1,3,2,0:T(8,128)(2,1)}) %all-gather.2.cloned.1.call-update) | async-done | bytes 4915216 | tf_op jit(solution)/shard_map/all_gather | solution.py:76
  99.3 17.9 %while.23 = (s32[]{:T(128)}, f32[8,8,2,128]{3,1,2,0:T(8,128)S(1)}, bf16[8,8,2,10,1920]{4,1,3,2,0:T(8,128)(2,1)}, s32[1920]{0:T(1024)S(1)}, s32[]{:T(128)}) while((s32[]{:T(128)}, f32[8,8,2,128]{3,1,2,0:T(8,128)S(1)}, bf16[8,8,2,10,1920]{4,1,3,2,0:T(8,128)(2,1)}, s32[1920]{0:T(1024)S(1)}, s32[]{:T(128)}) %tuple.59), condition=%wide.region_3.4_spmd.clone, body=%wide.region_1.3_spmd.clone.sunk | while | flops 237199360 | bytes 4333125 | solution.py:44
  99.3 1.2 bitcast_convert_fusion.5
  100.6 1.0 convolution_reduce_fusion.6
  101.6 1.2 bitcast_convert_fusion.5
  102.8 1.0 convolution_reduce_fusion.6
  103.8 1.2 bitcast_convert_fusion.5
  105.0 1.0 convolution_reduce_fusion.6
  106.0 1.2 bitcast_convert_fusion.5
  107.3 1.0 convolution_reduce_fusion.6
  108.3 1.2 bitcast_convert_fusion.5
  109.5 1.0 convolution_reduce_fusion.6
  110.5 1.2 bitcast_convert_fusion.5
  111.7 1.0 convolution_reduce_fusion.6
  112.7 1.2 bitcast_convert_fusion.5
  114.0 1.0 convolution_reduce_fusion.6
  115.0 1.2 bitcast_convert_fusion.5
  116.2 1.0 convolution_reduce_fusion.6
  117.2 32.4 %while.24 = (s32[]{:T(128)}, f32[4,2,8,2,128]{4,0,3,2,1:T(4,128)S(1)}, s32[4,2]{0,1:T(2,128)S(1)}, bf16[8,8,2,10,1920]{4,1,3,2,0:T(8,128)(2,1)}, f32[8]{0:T(128)...) while((s32[]{:T(128)}, ...), condition=%wide.region_7.8_spmd.clone.clone, body=%wide.region_4.7_spmd.clone.clone.sunk | while | flops 474415104 | bytes 8781057 | solution.py:56
  117.3 0.6 fusion.36
  121.6 1.4 bitcast_convert_fusion.6
  123.1 1.0 convolution_reduce_fusion.7
  124.1 1.0 convolution_reduce_fusion.8
  125.4 0.6 fusion.36
  129.7 1.4 bitcast_convert_fusion.6
  131.2 1.0 convolution_reduce_fusion.7
  132.2 1.0 convolution_reduce_fusion.8
  133.5 0.6 fusion.36
  137.7 1.4 bitcast_convert_fusion.6
  139.3 1.0 convolution_reduce_fusion.7
  140.3 1.0 convolution_reduce_fusion.8
  141.5 0.6 fusion.36
  145.8 1.4 bitcast_convert_fusion.6
  147.4 1.0 convolution_reduce_fusion.7
  148.4 1.0 convolution_reduce_fusion.8
  149.6 0.6 gather_fusion
  150.2 0.7 broadcast_select_fusion
  (66 shorter events, 2.7 us)
Async XLA Ops:
  6.5 53.0 %copy-start = (s32[16,2]{0,1:T(2,128)S(1)}, s32[16,2]{0,1:T(2,128)}, u32[]{:S(2)}) copy-start(s32[16,2]{0,1:T(2,128)} %param.11) | copy-start | bytes 388
  6.5 92.8 %all-gather.2.cloned.1.call-start = ((), (), s32[]{:S(2)}) async-start(), calls=%async_computation | async-start | bytes 6144000 | tf_op jit(solution)/shard_map/all_gather | solution.py:76
  8.8 8.9 %collective-permute-start = (bf16[2,1,1,2,10,1920]{5,3,4,2,1,0:T(2,128)(2,1)S(1)}, bf16[2,1,1,2,10,1920]{5,3,4,2,1,0:T(2,128)(2,1)S(1)}, u32[]{:S(2)}, u32[]{:S(2)}) collective-permute-start(bf16[2,1,1,2,10,1920]{5,3,4,2,1,0:T(2,128)(2,1)S(1)} %get-tuple-element.152), channel_id=1, source_target_pairs={{0,4},{4,0},{8,12},{12,8},{16,20},{20,16},{24,28},{28,24},{1,5},{5... | collective-permute-start | bytes 460808 | tf_op jit(solution)/shard_map/ppermute | solution.py:22
  11.8 12.4 %collective-permute-start.1 = (bf16[2,1,1,2,10,1920]{5,3,4,2,1,0:T(2,128)(2,1)S(1)}, bf16[2,1,1,2,10,1920]{5,3,4,2,1,0:T(2,128)(2,1)S(1)}, u32[]{:S(2)}, u32[]{:S(2)}) collective-permute-start(bf16[2,1,1,2,10,1920]{5,3,4,2,1,0:T(2,128)(2,1)S(1)} %get-tuple-element.151), channel_id=1, source_target_pairs={{0,8},{4,12},{8,0},{12,4},{16,24},{20,28},{24,16},{28,20},{1,9},{5... | collective-permute-start | bytes 460808 | tf_op jit(solution)/shard_map/ppermute | solution.py:22
  13.4 14.7 %collective-permute-start.2 = (bf16[2,1,1,2,10,1920]{5,3,4,2,1,0:T(2,128)(2,1)S(1)}, bf16[2,1,1,2,10,1920]{5,3,4,2,1,0:T(2,128)(2,1)S(1)}, u32[]{:S(2)}, u32[]{:S(2)}) collective-permute-start(bf16[2,1,1,2,10,1920]{5,3,4,2,1,0:T(2,128)(2,1)S(1)} %get-tuple-element.150), channel_id=1, source_target_pairs={{0,12},{4,8},{8,4},{12,0},{16,28},{20,24},{24,20},{28,16},{1,13},{... | collective-permute-start | bytes 460808 | tf_op jit(solution)/shard_map/ppermute | solution.py:22
  13.4 15.0 %collective-permute-start.3 = (bf16[2,1,1,2,10,1920]{5,3,4,2,1,0:T(2,128)(2,1)S(1)}, bf16[2,1,1,2,10,1920]{5,3,4,2,1,0:T(2,128)(2,1)S(1)}, u32[]{:S(2)}, u32[]{:S(2)}) collective-permute-start(bf16[2,1,1,2,10,1920]{5,3,4,2,1,0:T(2,128)(2,1)S(1)} %get-tuple-element.149), channel_id=1, source_target_pairs={{0,16},{4,20},{8,24},{12,28},{16,0},{20,4},{24,8},{28,12},{1,17},{... | collective-permute-start | bytes 460808 | tf_op jit(solution)/shard_map/ppermute | solution.py:22
  16.4 22.3 %collective-permute-start.4 = (bf16[2,1,1,2,10,1920]{5,3,4,2,1,0:T(2,128)(2,1)S(1)}, bf16[2,1,1,2,10,1920]{5,3,4,2,1,0:T(2,128)(2,1)S(1)}, u32[]{:S(2)}, u32[]{:S(2)}) collective-permute-start(bf16[2,1,1,2,10,1920]{5,3,4,2,1,0:T(2,128)(2,1)S(1)} %get-tuple-element.148), channel_id=1, source_target_pairs={{0,20},{4,16},{8,28},{12,24},{16,4},{20,0},{24,12},{28,8},{1,21},{... | collective-permute-start | bytes 460808 | tf_op jit(solution)/shard_map/ppermute | solution.py:22
  17.7 21.2 %collective-permute-start.5 = (bf16[2,1,1,2,10,1920]{5,3,4,2,1,0:T(2,128)(2,1)S(1)}, bf16[2,1,1,2,10,1920]{5,3,4,2,1,0:T(2,128)(2,1)}, u32[]{:S(2)}, u32[]{:S(2)}) collective-permute-start(bf16[2,1,1,2,10,1920]{5,3,4,2,1,0:T(2,128)(2,1)S(1)} %get-tuple-element.154), channel_id=1, source_target_pairs={{0,24},{4,28},{8,16},{12,20},{16,8},{20,12},{24,0},{28,4},{1,25},{... | collective-permute-start | bytes 460808 | tf_op jit(solution)/shard_map/ppermute | solution.py:22
  24.2 15.9 %collective-permute-start.6 = (bf16[2,1,1,2,10,1920]{5,3,4,2,1,0:T(2,128)(2,1)S(1)}, bf16[2,1,1,2,10,1920]{5,3,4,2,1,0:T(2,128)(2,1)}, u32[]{:S(2)}, u32[]{:S(2)}) collective-permute-start(bf16[2,1,1,2,10,1920]{5,3,4,2,1,0:T(2,128)(2,1)S(1)} %get-tuple-element.147), channel_id=1, source_target_pairs={{0,28},{4,24},{8,20},{12,16},{16,12},{20,8},{24,4},{28,0},{1,29},{... | collective-permute-start | bytes 460808 | tf_op jit(solution)/shard_map/ppermute | solution.py:22
  52.2 6.1 %copy-start.2 = (s32[1,8]{1,0:T(1,128)S(1)}, s32[1,8]{1,0:T(1,128)}, u32[]{:S(2)}) copy-start(s32[1,8]{1,0:T(1,128)} %param.9) | copy-start | bytes 100
  56.5 1.1 copy-start.1
Sparse Core Ops, SparseCore 0:
  57.7 41.5 all-gather.1
